TPU v7x, 512 devices: a whole 4x8x8 slice. The times are simulated.
512 devices in a mesh: rows: 32 (over x, z), cols: 16 (over y, core).
Axes of the slice: x: 4, y: 8, z: 8, core: 2. Of those that a mesh axis runs over, the one named last changes fastest.
Arguments:
- targets: float32 [3, 65536], P(None, 'rows'), may hold values from 0 to 1
- sources: float32 [3, 65536], P(None, 'cols'), may hold values from 0 to 1
- weights: float32 [65536], P('cols'), may hold values from 0.5 to 2
- counts: int32 [4096], P('cols'), may hold values from 8 to 16, as said below
- omega: bfloat16 [65536, 128], P('cols'), may hold values from -0.0234375 to 0.0234375
Outputs:
- basis: float32 [65536, 128], P('rows')
- projected: float32 [65536, 128], P(('cols', 'rows'))
Inputs may be any that keep to these rules, and one draw needn't show every extreme that they name: `counts`: some panel uses all 16 nodes.
All inputs are finite; a program needn't handle non-finite values.
Results may differ from a plain program's by a relative error of at most 0.0033.
Values may be sent and summed in bfloat16 or wider, within the bound.
No kernel may reach another device: no remote copies, remote signals or barrier semaphores. Data moves between devices by JAX's collectives and lax.ppermute only.
A program may use at most 64 MiB of HBM per device.

v0:
```python
import math
import jax
import jax.numpy as jnp
from jax import lax
from jax.sharding import PartitionSpec as P

wave_number = 160.0
separation = 2.0


def kernel_cols(targets, src_block, wts_block):
    diff_x = targets[0][None, :] - (src_block[0][:, None] + separation)
    diff_y = targets[1][None, :] - src_block[1][:, None]
    diff_z = targets[2][None, :] - src_block[2][:, None]
    distance = jnp.sqrt(diff_x * diff_x + diff_y * diff_y + diff_z * diff_z)
    return (wts_block[:, None] * jnp.cos(wave_number * distance) / distance).astype(jnp.bfloat16)


def contract_first(left, right):
    return lax.dot_general(
        left, right, (((0,), (0,)), ((), ())), preferred_element_type=jnp.float32
    )


def gram_of(rows_block):
    return jnp.dot(
        rows_block.T,
        rows_block,
        precision=lax.Precision.HIGHEST,
        preferred_element_type=jnp.float32,
    )


def solve_rows(rows_block, gram_matrix):
    lower_factor = jnp.linalg.cholesky(gram_matrix)
    return lax.linalg.triangular_solve(
        lower_factor, rows_block, left_side=False, lower=True, transpose_a=True
    )


def shards(targets, sources, weights, counts, omega):
    rows_here = targets.shape[1]
    cols_here = sources.shape[1]
    rank = omega.shape[1]
    panel_count = counts.shape[0]
    panel_size = cols_here // panel_count
    usable = (
        (lax.broadcasted_iota(jnp.int32, (panel_count, panel_size), 1) < counts[:, None])
        .reshape(-1)
        .astype(jnp.float32)
    )
    node_weight = weights * usable
    block_width = math.gcd(cols_here, 512)
    nblocks = cols_here // block_width
    src_blocks = sources.reshape(3, nblocks, block_width).transpose(1, 0, 2)
    wts_blocks = node_weight.reshape(nblocks, block_width)
    omega_blocks = omega.reshape(nblocks, block_width, rank)

    def sketch_turn(total, inputs):
        kernel_tile = kernel_cols(targets, inputs[0], inputs[1])
        return (total + contract_first(kernel_tile, inputs[2]), None)

    partial_sketch, _ = lax.scan(
        sketch_turn,
        jnp.zeros((rows_here, rank), jnp.float32),
        (src_blocks, wts_blocks, omega_blocks),
    )
    sketch = lax.psum(partial_sketch, "cols")
    gram_matrix = lax.psum(gram_of(sketch), "rows")
    ortho = solve_rows(sketch, gram_matrix)
    ortho_low = ortho.astype(jnp.bfloat16)
    row_devices = lax.axis_size("rows")
    own_count = cols_here // row_devices
    inner_width = math.gcd(lax.axis_size("rows") * own_count, 512)
    inner_blocks = lax.axis_size("rows") * own_count // inner_width
    sub_src_blocks = sources.reshape(3, inner_blocks, inner_width).transpose(1, 0, 2)
    sub_wts_blocks = node_weight.reshape(inner_blocks, inner_width)

    def project_block(inputs):
        kernel_tile = kernel_cols(targets, inputs[0], inputs[1])
        return jnp.dot(kernel_tile, ortho_low, preferred_element_type=jnp.float32)

    projected = lax.psum_scatter(
        lax.map(project_block, (sub_src_blocks, sub_wts_blocks)).reshape(
            lax.axis_size("rows") * own_count, rank
        ),
        "rows",
        scatter_dimension=0,
        tiled=True,
    )
    scaled = ortho * math.sqrt(rows_here * row_devices)
    return (scaled, projected)


def solution(mesh):
    return jax.shard_map(
        shards,
        mesh=mesh,
        in_specs=(P(None, "rows"), P(None, "cols"), P("cols"), P("cols"), P("cols", None)),
        out_specs=(P("rows", None), P(("cols", "rows"), None)),
        check_vma=False,
    )
```

profile of v0, /device:TPU:8, one launch (start us, length us, event | category | flops | bytes accessed | tf_op | source)
XLA Modules:
  0.0 845.4 jit_solution(1076110894502836828)
XLA Ops:
  8.9 154.4 %while.22 = (s32[]{:T(128)}, f32[2048,128]{1,0:T(8,128)S(1)}, f32[8,512]{1,0:T(8,128)S(1)}, f32[3,2048]{1,0:T(4,128)}, f32[8,3,512]{2,1,0:T(4,128)}, /*index=5*/...) while((s32[]{:T(128)}, f32[2048,128]{1,0:T(8,128)S(1)}, f32[8,512]{1,0:T(8,128)S(1)}, ...), condition=%wide.region_1.2_spmd.clone, body=%wide.region_0.1_spmd.clone.sunk | while | flops 281543168 | bytes 2327191 | solution.py:63
  9.7 0.9 fusion.36
  10.6 17.5 %convolution_add_fusion.2 = f32[2048,128]{1,0:T(8,128)S(1)} fusion(f32[512]{0:T(512)S(1)} %bitcast.85, f32[2048]{0:T(1024)S(1)} %bitcast.77, f32[512]{0:T(512)S(1)} %bitcast.84, f32[2048]{0:T(1024)S(1)} %bitcast.78, f32[512]{0:T(512)S(1)} %bitcast.83, f32[2048]{0:T(1024)S(1)} %bitcast.76, f32[512]{0:T(512)S(1)} %bitcast.89, ...), kind=kOutput, calls=%fused_computation.10.clone.1 | convolution fusion | flops 281542656 | bytes 2261505 | tf_op jit(solution)/shard_map/while/body/eval_jaxpr/dot_general | solution.py:20
  29.0 0.9 fusion.36
  29.9 17.5 %convolution_add_fusion.2 = f32[2048,128]{1,0:T(8,128)S(1)} fusion(f32[512]{0:T(512)S(1)} %bitcast.85, f32[2048]{0:T(1024)S(1)} %bitcast.77, f32[512]{0:T(512)S(1)} %bitcast.84, f32[2048]{0:T(1024)S(1)} %bitcast.78, f32[512]{0:T(512)S(1)} %bitcast.83, f32[2048]{0:T(1024)S(1)} %bitcast.76, f32[512]{0:T(512)S(1)} %bitcast.89, ...), kind=kOutput, calls=%fused_computation.10.clone.1 | convolution fusion | flops 281542656 | bytes 2261505 | tf_op jit(solution)/shard_map/while/body/eval_jaxpr/dot_general | solution.py:20
  48.2 0.9 fusion.36
  49.1 17.5 %convolution_add_fusion.2 = f32[2048,128]{1,0:T(8,128)S(1)} fusion(f32[512]{0:T(512)S(1)} %bitcast.85, f32[2048]{0:T(1024)S(1)} %bitcast.77, f32[512]{0:T(512)S(1)} %bitcast.84, f32[2048]{0:T(1024)S(1)} %bitcast.78, f32[512]{0:T(512)S(1)} %bitcast.83, f32[2048]{0:T(1024)S(1)} %bitcast.76, f32[512]{0:T(512)S(1)} %bitcast.89, ...), kind=kOutput, calls=%fused_computation.10.clone.1 | convolution fusion | flops 281542656 | bytes 2261505 | tf_op jit(solution)/shard_map/while/body/eval_jaxpr/dot_general | solution.py:20
  67.5 0.9 fusion.36
  68.4 17.5 %convolution_add_fusion.2 = f32[2048,128]{1,0:T(8,128)S(1)} fusion(f32[512]{0:T(512)S(1)} %bitcast.85, f32[2048]{0:T(1024)S(1)} %bitcast.77, f32[512]{0:T(512)S(1)} %bitcast.84, f32[2048]{0:T(1024)S(1)} %bitcast.78, f32[512]{0:T(512)S(1)} %bitcast.83, f32[2048]{0:T(1024)S(1)} %bitcast.76, f32[512]{0:T(512)S(1)} %bitcast.89, ...), kind=kOutput, calls=%fused_computation.10.clone.1 | convolution fusion | flops 281542656 | bytes 2261505 | tf_op jit(solution)/shard_map/while/body/eval_jaxpr/dot_general | solution.py:20
  86.8 0.9 fusion.36
  87.7 17.5 %convolution_add_fusion.2 = f32[2048,128]{1,0:T(8,128)S(1)} fusion(f32[512]{0:T(512)S(1)} %bitcast.85, f32[2048]{0:T(1024)S(1)} %bitcast.77, f32[512]{0:T(512)S(1)} %bitcast.84, f32[2048]{0:T(1024)S(1)} %bitcast.78, f32[512]{0:T(512)S(1)} %bitcast.83, f32[2048]{0:T(1024)S(1)} %bitcast.76, f32[512]{0:T(512)S(1)} %bitcast.89, ...), kind=kOutput, calls=%fused_computation.10.clone.1 | convolution fusion | flops 281542656 | bytes 2261505 | tf_op jit(solution)/shard_map/while/body/eval_jaxpr/dot_general | solution.py:20
  107.0 17.5 %convolution_add_fusion.2 = f32[2048,128]{1,0:T(8,128)S(1)} fusion(f32[512]{0:T(512)S(1)} %bitcast.85, f32[2048]{0:T(1024)S(1)} %bitcast.77, f32[512]{0:T(512)S(1)} %bitcast.84, f32[2048]{0:T(1024)S(1)} %bitcast.78, f32[512]{0:T(512)S(1)} %bitcast.83, f32[2048]{0:T(1024)S(1)} %bitcast.76, f32[512]{0:T(512)S(1)} %bitcast.89, ...), kind=kOutput, calls=%fused_computation.10.clone.1 | convolution fusion | flops 281542656 | bytes 2261505 | tf_op jit(solution)/shard_map/while/body/eval_jaxpr/dot_general | solution.py:20
  126.3 17.5 %convolution_add_fusion.2 = f32[2048,128]{1,0:T(8,128)S(1)} fusion(f32[512]{0:T(512)S(1)} %bitcast.85, f32[2048]{0:T(1024)S(1)} %bitcast.77, f32[512]{0:T(512)S(1)} %bitcast.84, f32[2048]{0:T(1024)S(1)} %bitcast.78, f32[512]{0:T(512)S(1)} %bitcast.83, f32[2048]{0:T(1024)S(1)} %bitcast.76, f32[512]{0:T(512)S(1)} %bitcast.89, ...), kind=kOutput, calls=%fused_computation.10.clone.1 | convolution fusion | flops 281542656 | bytes 2261505 | tf_op jit(solution)/shard_map/while/body/eval_jaxpr/dot_general | solution.py:20
  145.5 17.5 %convolution_add_fusion.2 = f32[2048,128]{1,0:T(8,128)S(1)} fusion(f32[512]{0:T(512)S(1)} %bitcast.85, f32[2048]{0:T(1024)S(1)} %bitcast.77, f32[512]{0:T(512)S(1)} %bitcast.84, f32[2048]{0:T(1024)S(1)} %bitcast.78, f32[512]{0:T(512)S(1)} %bitcast.83, f32[2048]{0:T(1024)S(1)} %bitcast.76, f32[512]{0:T(512)S(1)} %bitcast.89, ...), kind=kOutput, calls=%fused_computation.10.clone.1 | convolution fusion | flops 281542656 | bytes 2261505 | tf_op jit(solution)/shard_map/while/body/eval_jaxpr/dot_general | solution.py:20
  163.3 1.0 copy-done.2
  164.3 120.4 %all-reduce.3.cloned.1.call-done = f32[2048,128]{1,0:T(8,128)} async-done(((f32[2048,128]{1,0:T(8,128)}), f32[2048,128]{1,0:T(8,128)}) %all-reduce.3.cloned.1.call-update) | async-done | bytes 1048592 | tf_op jit(solution)/shard_map/psum | solution.py:68
  284.7 4.1 fusion.22
  288.9 155.6 %all-reduce.5.cloned.1.call-done = f32[128,128]{0,1:T(8,128)} async-done(((f32[128,128]{0,1:T(8,128)}), f32[128,128]{0,1:T(8,128)}) %all-reduce.5.cloned.1.call-update) | async-done | bytes 65552 | tf_op jit(solution)/shard_map/psum | solution.py:69
  444.5 0.9 copy.10
  446.3 11.7 %cholesky.16 = f32[128,128]{1,0:T(8,128)S(1)} custom-call(f32[128,128]{1,0:T(8,128)S(1)} %fusion.18), custom_call_target="Cholesky" | custom-call | tf_op jit(solution)/shard_map/jit(cholesky)/cholesky | solution.py:35
  459.3 9.8 %custom-call.6 = f32[1,128,128]{1,2,0:T(8,128)S(1)} custom-call(f32[1,128,128]{2,1,0:T(8,128)S(1)} %fusion.15), custom_call_target="InvertDiagBlocksLowerTriangular" | custom-call | tf_op jit(solution)/shard_map/triangular_solve | solution.py:36
  469.2 1.9 fusion.21
  471.1 144.9 %while.21 = (s32[]{:T(128)}, f32[8,512,128]{2,1,0:T(8,128)}, f32[8,512]{1,0:T(8,128)S(1)}, f32[3,2048]{1,0:T(4,128)S(1)}, f32[8,3,512]{2,1,0:T(4,128)}, /*index=...) while((s32[]{:T(128)}, f32[8,512,128]{2,1,0:T(8,128)}, f32[8,512]{1,0:T(8,128)S(1)}, ...), condition=%wide.region_7.8_spmd, body=%wide.region_6.7_spmd.sunk | while | flops 281018880 | bytes 885389 | solution.py:84
  472.0 17.3 %fusion.34 = f32[8,512,128]{2,1,0:T(8,128)} fusion(f32[8,512,128]{2,1,0:T(8,128)} %get-tuple-element.266, s32[]{:T(128)} %get-tuple-element.265, bf16[2048,128]{1,0:T(8,128)(2,1)S(1)} %get-tuple-element.280, f32[512]{0:T(512)S(1)} %bitcast.88, f32[2048]{0:T(1024)S(1)} %bitcast.80, f32[512]{0:T(512)S(1)} %bitcast.87, f32[2048]{0:T(1024)S(1)} %bitcast.81, ...), kind=kOutput, calls=%fused_computation.3.clone.1 | convolution fusion | flops 281018368 | bytes 819712 | tf_op jit(solution)/shard_map/while/body/eval_jaxpr/dot_general | solution.py:81
  490.1 17.3 %fusion.34 = f32[8,512,128]{2,1,0:T(8,128)} fusion(f32[8,512,128]{2,1,0:T(8,128)} %get-tuple-element.266, s32[]{:T(128)} %get-tuple-element.265, bf16[2048,128]{1,0:T(8,128)(2,1)S(1)} %get-tuple-element.280, f32[512]{0:T(512)S(1)} %bitcast.88, f32[2048]{0:T(1024)S(1)} %bitcast.80, f32[512]{0:T(512)S(1)} %bitcast.87, f32[2048]{0:T(1024)S(1)} %bitcast.81, ...), kind=kOutput, calls=%fused_computation.3.clone.1 | convolution fusion | flops 281018368 | bytes 819712 | tf_op jit(solution)/shard_map/while/body/eval_jaxpr/dot_general | solution.py:81
  508.2 17.3 %fusion.34 = f32[8,512,128]{2,1,0:T(8,128)} fusion(f32[8,512,128]{2,1,0:T(8,128)} %get-tuple-element.266, s32[]{:T(128)} %get-tuple-element.265, bf16[2048,128]{1,0:T(8,128)(2,1)S(1)} %get-tuple-element.280, f32[512]{0:T(512)S(1)} %bitcast.88, f32[2048]{0:T(1024)S(1)} %bitcast.80, f32[512]{0:T(512)S(1)} %bitcast.87, f32[2048]{0:T(1024)S(1)} %bitcast.81, ...), kind=kOutput, calls=%fused_computation.3.clone.1 | convolution fusion | flops 281018368 | bytes 819712 | tf_op jit(solution)/shard_map/while/body/eval_jaxpr/dot_general | solution.py:81
  526.3 17.3 %fusion.34 = f32[8,512,128]{2,1,0:T(8,128)} fusion(f32[8,512,128]{2,1,0:T(8,128)} %get-tuple-element.266, s32[]{:T(128)} %get-tuple-element.265, bf16[2048,128]{1,0:T(8,128)(2,1)S(1)} %get-tuple-element.280, f32[512]{0:T(512)S(1)} %bitcast.88, f32[2048]{0:T(1024)S(1)} %bitcast.80, f32[512]{0:T(512)S(1)} %bitcast.87, f32[2048]{0:T(1024)S(1)} %bitcast.81, ...), kind=kOutput, calls=%fused_computation.3.clone.1 | convolution fusion | flops 281018368 | bytes 819712 | tf_op jit(solution)/shard_map/while/body/eval_jaxpr/dot_general | solution.py:81
  544.4 17.2 %fusion.34 = f32[8,512,128]{2,1,0:T(8,128)} fusion(f32[8,512,128]{2,1,0:T(8,128)} %get-tuple-element.266, s32[]{:T(128)} %get-tuple-element.265, bf16[2048,128]{1,0:T(8,128)(2,1)S(1)} %get-tuple-element.280, f32[512]{0:T(512)S(1)} %bitcast.88, f32[2048]{0:T(1024)S(1)} %bitcast.80, f32[512]{0:T(512)S(1)} %bitcast.87, f32[2048]{0:T(1024)S(1)} %bitcast.81, ...), kind=kOutput, calls=%fused_computation.3.clone.1 | convolution fusion | flops 281018368 | bytes 819712 | tf_op jit(solution)/shard_map/while/body/eval_jaxpr/dot_general | solution.py:81
  562.5 17.2 %fusion.34 = f32[8,512,128]{2,1,0:T(8,128)} fusion(f32[8,512,128]{2,1,0:T(8,128)} %get-tuple-element.266, s32[]{:T(128)} %get-tuple-element.265, bf16[2048,128]{1,0:T(8,128)(2,1)S(1)} %get-tuple-element.280, f32[512]{0:T(512)S(1)} %bitcast.88, f32[2048]{0:T(1024)S(1)} %bitcast.80, f32[512]{0:T(512)S(1)} %bitcast.87, f32[2048]{0:T(1024)S(1)} %bitcast.81, ...), kind=kOutput, calls=%fused_computation.3.clone.1 | convolution fusion | flops 281018368 | bytes 819712 | tf_op jit(solution)/shard_map/while/body/eval_jaxpr/dot_general | solution.py:81
  580.6 17.2 %fusion.34 = f32[8,512,128]{2,1,0:T(8,128)} fusion(f32[8,512,128]{2,1,0:T(8,128)} %get-tuple-element.266, s32[]{:T(128)} %get-tuple-element.265, bf16[2048,128]{1,0:T(8,128)(2,1)S(1)} %get-tuple-element.280, f32[512]{0:T(512)S(1)} %bitcast.88, f32[2048]{0:T(1024)S(1)} %bitcast.80, f32[512]{0:T(512)S(1)} %bitcast.87, f32[2048]{0:T(1024)S(1)} %bitcast.81, ...), kind=kOutput, calls=%fused_computation.3.clone.1 | convolution fusion | flops 281018368 | bytes 819712 | tf_op jit(solution)/shard_map/while/body/eval_jaxpr/dot_general | solution.py:81
  598.7 17.3 %fusion.34 = f32[8,512,128]{2,1,0:T(8,128)} fusion(f32[8,512,128]{2,1,0:T(8,128)} %get-tuple-element.266, s32[]{:T(128)} %get-tuple-element.265, bf16[2048,128]{1,0:T(8,128)(2,1)S(1)} %get-tuple-element.280, f32[512]{0:T(512)S(1)} %bitcast.88, f32[2048]{0:T(1024)S(1)} %bitcast.80, f32[512]{0:T(512)S(1)} %bitcast.87, f32[2048]{0:T(1024)S(1)} %bitcast.81, ...), kind=kOutput, calls=%fused_computation.3.clone.1 | convolution fusion | flops 281018368 | bytes 819712 | tf_op jit(solution)/shard_map/while/body/eval_jaxpr/dot_general | solution.py:81
  616.0 222.9 %reduce-scatter.2.cloned.1.call-done = f32[128,128]{1,0:T(8,128)} async-done(((f32[4096,128]{1,0:T(8,128)}), f32[128,128]{1,0:T(8,128)}) %reduce-scatter.2.cloned.1.call-update) | async-done | bytes 65552 | tf_op jit(solution)/shard_map/reduce_scatter | solution.py:83
  (64 shorter events, 20.0 us)
Async XLA Ops:
  7.2 277.5 %all-reduce.3.cloned.1.call-start = ((), (), s32[]{:S(2)}) async-start(), calls=%async_computation.1 | async-start | bytes 2097152 | tf_op jit(solution)/shard_map/psum | solution.py:68
  163.3 1.0 copy-start.2
  164.3 280.2 %all-reduce.5.cloned.1.call-start = ((), (), s32[]{:S(2)}) async-start(), calls=%async_computation.2 | async-start | bytes 131072 | tf_op jit(solution)/shard_map/psum | solution.py:69
  284.7 184.5 %copy-start = (f32[2048,128]{1,0:T(8,128)S(1)}, f32[2048,128]{1,0:T(8,128)}, u32[]{:S(2)}) copy-start(f32[2048,128]{1,0:T(8,128)} %all-reduce.3.cloned.1.call-done) | copy-start | bytes 3145732
  288.8 182.3 %copy-start.1 = (f32[3,2048]{1,0:T(4,128)S(1)}, f32[3,2048]{1,0:T(4,128)}, u32[]{:S(2)}) copy-start(f32[3,2048]{1,0:T(4,128)} %get-tuple-element.291) | copy-start | bytes 73732
  288.8 550.0 %reduce-scatter.2.cloned.1.call-start = ((), (), s32[]{:S(2)}) async-start(), calls=%async_computation.3 | async-start | bytes 2162688 | tf_op jit(solution)/shard_map/reduce_scatter | solution.py:83
Sparse Core Ops, SparseCore 0:
  164.4 120.2 all-reduce.2
  289.0 155.4 all-reduce.4
  616.1 222.6 reduce-scatter.1
where the time goes:
time: 847 us; the launch traced here: 845 us
  waiting for transfers between devices  499 us (59%)
  matrix products  284 us (34%)
  other arithmetic  38.3 us (5%)
  between operations  13.8 us (2%)
  local copies, waits for them, and re-layouts  9.44 us (1%)
    reduce_scatter x1, waiting for transfers between devices, shards(): lax.psum_scatter(lax.map(project_block, (sub_src_blocks, sub_wts_blocks))...  223 us
    psum x1, waiting for transfers between devices, shards(): gram_matrix = lax.psum(gram_of(sketch), 'rows')  156 us
    dot_general x8, matrix products, contract_first(): lax.dot_general(left, right, (((0,), (0,)), ((), ())), preferred_element_...  140 us
    dot_general x8, matrix products, project_block(): return jnp.dot(kernel_tile, ortho_low, preferred_element_type=jnp.float32)  138 us
    psum x1, waiting for transfers between devices, shards(): sketch = lax.psum(partial_sketch, 'cols')  120 us
  transfers between devices with their start and end apart: 3, of which 3 were waited for; matrix products, arithmetic and copies ran while one was open for 0% of the time, Pallas kernels for 0%

commit v1 on v0

--- a/solution.py
+++ b/solution.py
@@ -65,7 +65,9 @@
         jnp.zeros((rows_here, rank), jnp.float32),
         (src_blocks, wts_blocks, omega_blocks),
     )
-    sketch = lax.psum(partial_sketch, "cols")
+    sketch = partial_sketch
+    for hop in (1, 2, 4, 8):
+        sketch = sketch + lax.ppermute(sketch, "cols", [(dev, dev ^ hop) for dev in range(16)])
     gram_matrix = lax.psum(gram_of(sketch), "rows")
     ortho = solve_rows(sketch, gram_matrix)
     ortho_low = ortho.astype(jnp.bfloat16)

time: 847 us -> 879 us (1.038); the launches traced: 845 us -> 865 us
  starting transfers between devices: 0.12 us -> 14.6 us
    psum x1 -> x0, waiting for transfers between devices: 120 us -> none  [shards(): sketch = lax.psum(partial_sketch, 'cols')]
    ppermute x0 -> x4, waiting for transfers between devices: none -> 109 us  [shards(): lax.ppermute(sketch, 'cols', [(dev, dev ^ hop) for dev in range(16)])]
    ppermute x0 -> x4, starting transfers between devices: none -> 14.5 us  [shards(): lax.ppermute(sketch, 'cols', [(dev, dev ^ hop) for dev in range(16)])]
    psum x1, waiting for transfers between devices: 156 us -> 166 us  [shards(): gram_matrix = lax.psum(gram_of(sketch), 'rows')]
  transfers between devices with their start and end apart: 3 -> 6, of which waited for: 3 -> 6; matrix products, arithmetic and copies ran while one was open for 0% -> 0% of each run, Pallas kernels for 0% -> 0%
where the time goes in v1:
time: 879 us; the launch traced here: 865 us
  waiting for transfers between devices  498 us (57%)
  matrix products  283 us (32%)
  other arithmetic  38.7 us (4%)
  starting transfers between devices  14.6 us (2%)
  between operations  14.5 us (2%)
    reduce_scatter x1, waiting for transfers between devices, shards(): lax.psum_scatter(lax.map(project_block, (sub_src_blocks, sub_wts_blocks))...  223 us
    psum x1, waiting for transfers between devices, shards(): gram_matrix = lax.psum(gram_of(sketch), 'rows')  166 us
    dot_general x8, matrix products, contract_first(): lax.dot_general(left, right, (((0,), (0,)), ((), ())), preferred_element_...  140 us
    dot_general x8, matrix products, project_block(): return jnp.dot(kernel_tile, ortho_low, preferred_element_type=jnp.float32)  138 us
    ppermute x4, waiting for transfers between devices, shards(): lax.ppermute(sketch, 'cols', [(dev, dev ^ hop) for dev in range(16)])  109 us
  transfers between devices with their start and end apart: 6, of which 6 were waited for; matrix products, arithmetic and copies ran while one was open for 0% of the time, Pallas kernels for 0%

profile of v1, /device:TPU:8, one launch (start us, length us, event | category | flops | bytes accessed | tf_op | source)
XLA Modules:
  0.0 864.9 jit_solution(2708519385734616404)
XLA Ops:
  8.9 161.8 %while.22 = (s32[]{:T(128)}, f32[2048,128]{1,0:T(8,128)S(1)}, f32[8,512]{1,0:T(8,128)S(1)}, f32[3,2048]{1,0:T(4,128)}, f32[8,3,512]{2,1,0:T(4,128)}, /*index=5*/...) while((s32[]{:T(128)}, f32[2048,128]{1,0:T(8,128)S(1)}, f32[8,512]{1,0:T(8,128)S(1)}, ...), condition=%wide.region_1.2_spmd.clone, body=%wide.region_0.1_spmd.clone.sunk | while | flops 281543168 | bytes 2327191 | solution.py:63
  10.6 17.5 %convolution_add_fusion.2 = f32[2048,128]{1,0:T(8,128)S(1)} fusion(f32[512]{0:T(512)S(1)} %bitcast.85, f32[2048]{0:T(1024)S(1)} %bitcast.77, f32[512]{0:T(512)S(1)} %bitcast.84, f32[2048]{0:T(1024)S(1)} %bitcast.78, f32[512]{0:T(512)S(1)} %bitcast.83, f32[2048]{0:T(1024)S(1)} %bitcast.76, f32[512]{0:T(512)S(1)} %bitcast.89, ...), kind=kOutput, calls=%fused_computation.10.clone.1 | convolution fusion | flops 281542656 | bytes 2261505 | tf_op jit(solution)/shard_map/while/body/eval_jaxpr/dot_general | solution.py:20
  29.9 17.5 %convolution_add_fusion.2 = f32[2048,128]{1,0:T(8,128)S(1)} fusion(f32[512]{0:T(512)S(1)} %bitcast.85, f32[2048]{0:T(1024)S(1)} %bitcast.77, f32[512]{0:T(512)S(1)} %bitcast.84, f32[2048]{0:T(1024)S(1)} %bitcast.78, f32[512]{0:T(512)S(1)} %bitcast.83, f32[2048]{0:T(1024)S(1)} %bitcast.76, f32[512]{0:T(512)S(1)} %bitcast.89, ...), kind=kOutput, calls=%fused_computation.10.clone.1 | convolution fusion | flops 281542656 | bytes 2261505 | tf_op jit(solution)/shard_map/while/body/eval_jaxpr/dot_general | solution.py:20
  49.1 17.5 %convolution_add_fusion.2 = f32[2048,128]{1,0:T(8,128)S(1)} fusion(f32[512]{0:T(512)S(1)} %bitcast.85, f32[2048]{0:T(1024)S(1)} %bitcast.77, f32[512]{0:T(512)S(1)} %bitcast.84, f32[2048]{0:T(1024)S(1)} %bitcast.78, f32[512]{0:T(512)S(1)} %bitcast.83, f32[2048]{0:T(1024)S(1)} %bitcast.76, f32[512]{0:T(512)S(1)} %bitcast.89, ...), kind=kOutput, calls=%fused_computation.10.clone.1 | convolution fusion | flops 281542656 | bytes 2261505 | tf_op jit(solution)/shard_map/while/body/eval_jaxpr/dot_general | solution.py:20
  68.4 17.5 %convolution_add_fusion.2 = f32[2048,128]{1,0:T(8,128)S(1)} fusion(f32[512]{0:T(512)S(1)} %bitcast.85, f32[2048]{0:T(1024)S(1)} %bitcast.77, f32[512]{0:T(512)S(1)} %bitcast.84, f32[2048]{0:T(1024)S(1)} %bitcast.78, f32[512]{0:T(512)S(1)} %bitcast.83, f32[2048]{0:T(1024)S(1)} %bitcast.76, f32[512]{0:T(512)S(1)} %bitcast.89, ...), kind=kOutput, calls=%fused_computation.10.clone.1 | convolution fusion | flops 281542656 | bytes 2261505 | tf_op jit(solution)/shard_map/while/body/eval_jaxpr/dot_general | solution.py:20
  87.7 17.5 %convolution_add_fusion.2 = f32[2048,128]{1,0:T(8,128)S(1)} fusion(f32[512]{0:T(512)S(1)} %bitcast.85, f32[2048]{0:T(1024)S(1)} %bitcast.77, f32[512]{0:T(512)S(1)} %bitcast.84, f32[2048]{0:T(1024)S(1)} %bitcast.78, f32[512]{0:T(512)S(1)} %bitcast.83, f32[2048]{0:T(1024)S(1)} %bitcast.76, f32[512]{0:T(512)S(1)} %bitcast.89, ...), kind=kOutput, calls=%fused_computation.10.clone.1 | convolution fusion | flops 281542656 | bytes 2261505 | tf_op jit(solution)/shard_map/while/body/eval_jaxpr/dot_general | solution.py:20
  107.0 17.5 %convolution_add_fusion.2 = f32[2048,128]{1,0:T(8,128)S(1)} fusion(f32[512]{0:T(512)S(1)} %bitcast.85, f32[2048]{0:T(1024)S(1)} %bitcast.77, f32[512]{0:T(512)S(1)} %bitcast.84, f32[2048]{0:T(1024)S(1)} %bitcast.78, f32[512]{0:T(512)S(1)} %bitcast.83, f32[2048]{0:T(1024)S(1)} %bitcast.76, f32[512]{0:T(512)S(1)} %bitcast.89, ...), kind=kOutput, calls=%fused_computation.10.clone.1 | convolution fusion | flops 281542656 | bytes 2261505 | tf_op jit(solution)/shard_map/while/body/eval_jaxpr/dot_general | solution.py:20
  126.3 17.5 %convolution_add_fusion.2 = f32[2048,128]{1,0:T(8,128)S(1)} fusion(f32[512]{0:T(512)S(1)} %bitcast.85, f32[2048]{0:T(1024)S(1)} %bitcast.77, f32[512]{0:T(512)S(1)} %bitcast.84, f32[2048]{0:T(1024)S(1)} %bitcast.78, f32[512]{0:T(512)S(1)} %bitcast.83, f32[2048]{0:T(1024)S(1)} %bitcast.76, f32[512]{0:T(512)S(1)} %bitcast.89, ...), kind=kOutput, calls=%fused_computation.10.clone.1 | convolution fusion | flops 281542656 | bytes 2261505 | tf_op jit(solution)/shard_map/while/body/eval_jaxpr/dot_general | solution.py:20
  145.5 17.5 %convolution_add_fusion.2 = f32[2048,128]{1,0:T(8,128)S(1)} fusion(f32[512]{0:T(512)S(1)} %bitcast.85, f32[2048]{0:T(1024)S(1)} %bitcast.77, f32[512]{0:T(512)S(1)} %bitcast.84, f32[2048]{0:T(1024)S(1)} %bitcast.78, f32[512]{0:T(512)S(1)} %bitcast.83, f32[2048]{0:T(1024)S(1)} %bitcast.76, f32[512]{0:T(512)S(1)} %bitcast.89, ...), kind=kOutput, calls=%fused_computation.10.clone.1 | convolution fusion | flops 281542656 | bytes 2261505 | tf_op jit(solution)/shard_map/while/body/eval_jaxpr/dot_general | solution.py:20
  170.7 1.9 collective-permute-start
  172.6 2.6 collective-permute-done
  175.3 7.7 collective-permute-start.1
  183.0 23.4 %collective-permute-done.1 = f32[2048,128]{1,0:T(8,128)S(1)} collective-permute-done((f32[2048,128]{1,0:T(8,128)S(1)}, f32[2048,128]{1,0:T(8,128)S(1)}, u32[]{:S(2)}, u32[]{:S(2)}) %collective-permute-start.1) | collective-permute-done | bytes 1048608 | tf_op jit(solution)/shard_map/ppermute | solution.py:70
  206.6 1.9 collective-permute-start.2
  208.5 44.9 %collective-permute-done.2 = f32[2048,128]{1,0:T(8,128)S(1)} collective-permute-done((f32[2048,128]{1,0:T(8,128)S(1)}, f32[2048,128]{1,0:T(8,128)S(1)}, u32[]{:S(2)}, u32[]{:S(2)}) %collective-permute-start.2) | collective-permute-done | bytes 1048608 | tf_op jit(solution)/shard_map/ppermute | solution.py:70
  253.5 3.0 collective-permute-start.3
  256.5 37.8 %collective-permute-done.3 = f32[2048,128]{1,0:T(8,128)S(1)} collective-permute-done((f32[2048,128]{1,0:T(8,128)S(1)}, f32[2048,128]{1,0:T(8,128)S(1)}, u32[]{:S(2)}, u32[]{:S(2)}) %collective-permute-start.3) | collective-permute-done | bytes 1048608 | tf_op jit(solution)/shard_map/ppermute | solution.py:70
  294.5 2.4 fusion.22
  297.0 166.3 %all-reduce.2.cloned.1.call-done = f32[128,128]{0,1:T(8,128)} async-done(((f32[128,128]{0,1:T(8,128)}), f32[128,128]{0,1:T(8,128)}) %all-reduce.2.cloned.1.call-update) | async-done | bytes 65552 | tf_op jit(solution)/shard_map/psum | solution.py:71
  465.1 11.7 %cholesky.16 = f32[128,128]{1,0:T(8,128)S(1)} custom-call(f32[128,128]{1,0:T(8,128)S(1)} %fusion.18), custom_call_target="Cholesky" | custom-call | tf_op jit(solution)/shard_map/jit(cholesky)/cholesky | solution.py:35
  478.1 9.8 %custom-call.6 = f32[1,128,128]{1,2,0:T(8,128)S(1)} custom-call(f32[1,128,128]{2,1,0:T(8,128)S(1)} %fusion.15), custom_call_target="InvertDiagBlocksLowerTriangular" | custom-call | tf_op jit(solution)/shard_map/triangular_solve | solution.py:36
  488.0 1.9 fusion.21
  489.9 144.9 %while.21 = (s32[]{:T(128)}, f32[8,512,128]{2,1,0:T(8,128)}, f32[8,512]{1,0:T(8,128)S(1)}, f32[3,2048]{1,0:T(4,128)S(1)}, f32[8,3,512]{2,1,0:T(4,128)}, /*index=...) while((s32[]{:T(128)}, f32[8,512,128]{2,1,0:T(8,128)}, f32[8,512]{1,0:T(8,128)S(1)}, ...), condition=%wide.region_6.7_spmd, body=%wide.region_5.6_spmd.sunk | while | flops 281018880 | bytes 885389 | solution.py:86
  490.8 17.3 %fusion.34 = f32[8,512,128]{2,1,0:T(8,128)} fusion(f32[8,512,128]{2,1,0:T(8,128)} %get-tuple-element.266, s32[]{:T(128)} %get-tuple-element.265, bf16[2048,128]{1,0:T(8,128)(2,1)S(1)} %get-tuple-element.280, f32[512]{0:T(512)S(1)} %bitcast.88, f32[2048]{0:T(1024)S(1)} %bitcast.80, f32[512]{0:T(512)S(1)} %bitcast.87, f32[2048]{0:T(1024)S(1)} %bitcast.81, ...), kind=kOutput, calls=%fused_computation.3.clone.1 | convolution fusion | flops 281018368 | bytes 819712 | tf_op jit(solution)/shard_map/while/body/eval_jaxpr/dot_general | solution.py:83
  508.9 17.3 %fusion.34 = f32[8,512,128]{2,1,0:T(8,128)} fusion(f32[8,512,128]{2,1,0:T(8,128)} %get-tuple-element.266, s32[]{:T(128)} %get-tuple-element.265, bf16[2048,128]{1,0:T(8,128)(2,1)S(1)} %get-tuple-element.280, f32[512]{0:T(512)S(1)} %bitcast.88, f32[2048]{0:T(1024)S(1)} %bitcast.80, f32[512]{0:T(512)S(1)} %bitcast.87, f32[2048]{0:T(1024)S(1)} %bitcast.81, ...), kind=kOutput, calls=%fused_computation.3.clone.1 | convolution fusion | flops 281018368 | bytes 819712 | tf_op jit(solution)/shard_map/while/body/eval_jaxpr/dot_general | solution.py:83
  527.0 17.3 %fusion.34 = f32[8,512,128]{2,1,0:T(8,128)} fusion(f32[8,512,128]{2,1,0:T(8,128)} %get-tuple-element.266, s32[]{:T(128)} %get-tuple-element.265, bf16[2048,128]{1,0:T(8,128)(2,1)S(1)} %get-tuple-element.280, f32[512]{0:T(512)S(1)} %bitcast.88, f32[2048]{0:T(1024)S(1)} %bitcast.80, f32[512]{0:T(512)S(1)} %bitcast.87, f32[2048]{0:T(1024)S(1)} %bitcast.81, ...), kind=kOutput, calls=%fused_computation.3.clone.1 | convolution fusion | flops 281018368 | bytes 819712 | tf_op jit(solution)/shard_map/while/body/eval_jaxpr/dot_general | solution.py:83
  545.1 17.3 %fusion.34 = f32[8,512,128]{2,1,0:T(8,128)} fusion(f32[8,512,128]{2,1,0:T(8,128)} %get-tuple-element.266, s32[]{:T(128)} %get-tuple-element.265, bf16[2048,128]{1,0:T(8,128)(2,1)S(1)} %get-tuple-element.280, f32[512]{0:T(512)S(1)} %bitcast.88, f32[2048]{0:T(1024)S(1)} %bitcast.80, f32[512]{0:T(512)S(1)} %bitcast.87, f32[2048]{0:T(1024)S(1)} %bitcast.81, ...), kind=kOutput, calls=%fused_computation.3.clone.1 | convolution fusion | flops 281018368 | bytes 819712 | tf_op jit(solution)/shard_map/while/body/eval_jaxpr/dot_general | solution.py:83
  563.2 17.3 %fusion.34 = f32[8,512,128]{2,1,0:T(8,128)} fusion(f32[8,512,128]{2,1,0:T(8,128)} %get-tuple-element.266, s32[]{:T(128)} %get-tuple-element.265, bf16[2048,128]{1,0:T(8,128)(2,1)S(1)} %get-tuple-element.280, f32[512]{0:T(512)S(1)} %bitcast.88, f32[2048]{0:T(1024)S(1)} %bitcast.80, f32[512]{0:T(512)S(1)} %bitcast.87, f32[2048]{0:T(1024)S(1)} %bitcast.81, ...), kind=kOutput, calls=%fused_computation.3.clone.1 | convolution fusion | flops 281018368 | bytes 819712 | tf_op jit(solution)/shard_map/while/body/eval_jaxpr/dot_general | solution.py:83
  581.3 17.3 %fusion.34 = f32[8,512,128]{2,1,0:T(8,128)} fusion(f32[8,512,128]{2,1,0:T(8,128)} %get-tuple-element.266, s32[]{:T(128)} %get-tuple-element.265, bf16[2048,128]{1,0:T(8,128)(2,1)S(1)} %get-tuple-element.280, f32[512]{0:T(512)S(1)} %bitcast.88, f32[2048]{0:T(1024)S(1)} %bitcast.80, f32[512]{0:T(512)S(1)} %bitcast.87, f32[2048]{0:T(1024)S(1)} %bitcast.81, ...), kind=kOutput, calls=%fused_computation.3.clone.1 | convolution fusion | flops 281018368 | bytes 819712 | tf_op jit(solution)/shard_map/while/body/eval_jaxpr/dot_general | solution.py:83
  599.4 17.2 %fusion.34 = f32[8,512,128]{2,1,0:T(8,128)} fusion(f32[8,512,128]{2,1,0:T(8,128)} %get-tuple-element.266, s32[]{:T(128)} %get-tuple-element.265, bf16[2048,128]{1,0:T(8,128)(2,1)S(1)} %get-tuple-element.280, f32[512]{0:T(512)S(1)} %bitcast.88, f32[2048]{0:T(1024)S(1)} %bitcast.80, f32[512]{0:T(512)S(1)} %bitcast.87, f32[2048]{0:T(1024)S(1)} %bitcast.81, ...), kind=kOutput, calls=%fused_computation.3.clone.1 | convolution fusion | flops 281018368 | bytes 819712 | tf_op jit(solution)/shard_map/while/body/eval_jaxpr/dot_general | solution.py:83
  617.5 17.3 %fusion.34 = f32[8,512,128]{2,1,0:T(8,128)} fusion(f32[8,512,128]{2,1,0:T(8,128)} %get-tuple-element.266, s32[]{:T(128)} %get-tuple-element.265, bf16[2048,128]{1,0:T(8,128)(2,1)S(1)} %get-tuple-element.280, f32[512]{0:T(512)S(1)} %bitcast.88, f32[2048]{0:T(1024)S(1)} %bitcast.80, f32[512]{0:T(512)S(1)} %bitcast.87, f32[2048]{0:T(1024)S(1)} %bitcast.81, ...), kind=kOutput, calls=%fused_computation.3.clone.1 | convolution fusion | flops 281018368 | bytes 819712 | tf_op jit(solution)/shard_map/while/body/eval_jaxpr/dot_general | solution.py:83
  634.8 222.9 %reduce-scatter.2.cloned.1.call-done = f32[128,128]{1,0:T(8,128)} async-done(((f32[4096,128]{1,0:T(8,128)}), f32[128,128]{1,0:T(8,128)}) %reduce-scatter.2.cloned.1.call-update) | async-done | bytes 65552 | tf_op jit(solution)/shard_map/reduce_scatter | solution.py:85
  (69 shorter events, 25.8 us)
Async XLA Ops:
  7.2 456.1 %all-reduce.2.cloned.1.call-start = ((), (), s32[]{:S(2)}) async-start(), calls=%async_computation.1 | async-start | bytes 131072 | tf_op jit(solution)/shard_map/psum | solution.py:71
  170.7 4.6 collective-permute-start
  175.3 31.2 %collective-permute-start.1 = (f32[2048,128]{1,0:T(8,128)S(1)}, f32[2048,128]{1,0:T(8,128)S(1)}, u32[]{:S(2)}, u32[]{:S(2)}) collective-permute-start(f32[2048,128]{1,0:T(8,128)S(1)} %add.70), channel_id=1, source_target_pairs={{0,2},{1,3},{2,0},{3,1},{4,6},{5,7},{6,4},{7,5},{8,10},{9,11},{10,... | collective-permute-start | bytes 3145736 | tf_op jit(solution)/shard_map/ppermute | solution.py:70
  206.6 46.8 %collective-permute-start.2 = (f32[2048,128]{1,0:T(8,128)S(1)}, f32[2048,128]{1,0:T(8,128)S(1)}, u32[]{:S(2)}, u32[]{:S(2)}) collective-permute-start(f32[2048,128]{1,0:T(8,128)S(1)} %add.71), channel_id=1, source_target_pairs={{0,4},{1,5},{2,6},{3,7},{4,0},{5,1},{6,2},{7,3},{8,12},{9,13},{10,... | collective-permute-start | bytes 3145736 | tf_op jit(solution)/shard_map/ppermute | solution.py:70
  253.5 40.8 %collective-permute-start.3 = (f32[2048,128]{1,0:T(8,128)S(1)}, f32[2048,128]{1,0:T(8,128)S(1)}, u32[]{:S(2)}, u32[]{:S(2)}) collective-permute-start(f32[2048,128]{1,0:T(8,128)S(1)} %add.72), channel_id=1, source_target_pairs={{0,8},{1,9},{2,10},{3,11},{4,12},{5,13},{6,14},{7,15},{8,0},{9,1},... | collective-permute-start | bytes 3145736 | tf_op jit(solution)/shard_map/ppermute | solution.py:70
  296.9 193.0 %copy-start = (f32[3,2048]{1,0:T(4,128)S(1)}, f32[3,2048]{1,0:T(4,128)}, u32[]{:S(2)}) copy-start(f32[3,2048]{1,0:T(4,128)} %get-tuple-element.292) | copy-start | bytes 73732
  296.9 560.7 %reduce-scatter.2.cloned.1.call-start = ((), (), s32[]{:S(2)}) async-start(), calls=%async_computation.2 | async-start | bytes 2162688 | tf_op jit(solution)/shard_map/reduce_scatter | solution.py:85
Sparse Core Ops, SparseCore 0:
  297.1 166.1 all-reduce.1
  634.9 222.6 reduce-scatter.1
